TPU v7x, 128 devices: a whole 4x4x4 slice. The times are simulated.
128 devices in a mesh: col: 8 (over x, y_lo), sec: 16 (over y_hi, z, core).
Axes of the slice: x: 4, y: 4 (y_hi: 2, y_lo: 2; y = y_hi * 2 + y_lo), z: 4, core: 2. Of those that a mesh axis runs over, the one named last changes fastest.
Arguments:
- thermal_state: float32 [128, 128, 256], P('sec', 'col'), may hold values from -6 to 6
- flow_vector: float32 [2, 128, 128, 256], P(None, 'sec', 'col'), may hold values from -5 to 5
- vertical_spreading: float32 [128, 128, 256], P('sec', 'col'), may hold values from 0.05 to 0.5
- solute_fields: float32 [32, 128, 128, 256], P('sec', None, 'col'), may hold values from 0.1 to 2
- linear_exchange_speeds: float32 [32, 32], replicated, may hold values from -1 to 1
- newton_preconditioner: float32 [32, 32], replicated, may hold values from -0.6 to 1.2
- absorption_speed: float32 [32], replicated, may hold values from 0.2 to 2
- water_indicator: int32 [128, 256], P('col'), may hold values from 0 to 1, as said below
Outputs:
- thermal_revised: float32 [128, 128, 256], P('sec', 'col')
- velocity_next: float32 [2, 128, 128, 256], P(None, 'sec', 'col')
- diffusivity_next: float32 [128, 128, 256], P('sec', 'col')
- solute_revised: float32 [32, 128, 128, 256], P('sec', None, 'col')
Inputs may be any that keep to these rules, and one draw needn't show every extreme that they name: `water_indicator`: in each block of 16 consecutive longitudes, between 1536 and 3072 columns are wet, and some block holds exactly 3072 wet columns.
All inputs are finite; a program needn't handle non-finite values.
Results may differ from a plain program's by a relative error of at most 0.0001.
Values sent between devices are 32-bit elements; how exact they have to be, the bound alone decides.
A program may use at most 128 MiB of HBM per device.

v0:
```python
import jax
import jax.numpy as jnp
from jax import lax
from jax.sharding import PartitionSpec as P

NEWTON = 2


CORIOLIS = 0.8
MIXING = 0.1
ADVECTION = 0.2
VERTICAL_MIX = 0.3
WATER_ABSORB = 0.02
PIGMENT_ABSORB = 0.06
CHLOROPHYLL_WARM = 10.0


def shifted(block, axis, distance):
    devices = range(lax.axis_size(axis))
    route = [(i - distance, i) for i in devices if i - distance in devices]
    return lax.ppermute(block, axis, route)


def with_halo(cells, sides, width):
    for axis, dim in sides:
        count = lax.axis_size(axis)
        head = lax.slice_in_dim(cells, 0, width, axis=dim)
        tail = lax.slice_in_dim(cells, cells.shape[dim] - width, cells.shape[dim], axis=dim)
        cells = jnp.concatenate(
            [
                lax.ppermute(tail, axis, [(i, (i + 1) % count) for i in range(count)]),
                cells,
                lax.ppermute(head, axis, [((i + 1) % count, i) for i in range(count)]),
            ],
            axis=dim,
        )
    return cells


def sent_together(arrays, axis, dim, along):
    ends, at = ([], 0)
    for a in arrays[:-1]:
        at += a.shape[along]
        ends.append(at)
    both = jnp.concatenate(arrays, axis=along)
    return tuple(jnp.split(lax.all_gather(both, axis, axis=dim, tiled=True), ends, axis=along))


def chemical_change(center, eastern, western, east_flow, north_flow):
    northern = jnp.concatenate([center[..., 1:], center[..., -1:]], axis=-1)
    southern = jnp.concatenate([center[..., :1], center[..., :-1]], axis=-1)
    laplace = eastern + western + northern + southern - 4.0 * center
    return MIXING * laplace - 0.5 * ADVECTION * (
        east_flow * (eastern - western) + north_flow * (northern - southern)
    )


def column_mixing(field, kappa):
    weights = VERTICAL_MIX * kappa[:-1]
    fluxes = weights[None] * (field[:, 1:] - field[:, :-1])
    zeros = jnp.zeros_like(fluxes[:, :1])
    return jnp.concatenate([fluxes, zeros], axis=1) - jnp.concatenate([zeros, fluxes], axis=1)


def react(start, linear_exchange_speeds, newton_preconditioner, absorption_speed):
    rates = absorption_speed.reshape((-1,) + (1,) * (start.ndim - 1))
    current = start
    for step in range(NEWTON):
        linear = jnp.einsum(
            "ij,jlc->ilc", linear_exchange_speeds, current, precision=lax.Precision.HIGHEST
        )
        square = current * current
        rate = linear - rates * square / (1.0 + square)
        misfit = current - start - rate
        current = current - jnp.einsum(
            "ij,jlc->ilc", newton_preconditioner, misfit, precision=lax.Precision.HIGHEST
        )
    return current


def heating(pigment_tracer, shortwave):
    square = pigment_tracer * pigment_tracer
    absorb = WATER_ABSORB + PIGMENT_ABSORB * square / (1.0 + square)
    depth = jnp.cumsum(absorb, axis=0)
    return shortwave * (jnp.exp(-(depth - absorb)) - jnp.exp(-depth))


def sun_height(columns, lat_count):
    latitude = jnp.pi * ((columns % lat_count).astype(jnp.float32) + 0.5) / lat_count - jnp.pi / 2
    return jnp.cos(latitude)[None, :]


def on_device(
    thermal_state,
    flow_vector,
    vertical_spreading,
    solute_fields,
    linear_exchange_speeds,
    newton_preconditioner,
    absorption_speed,
    water_indicator,
):
    sections = lax.axis_size("sec")
    section = lax.axis_index("sec")
    held_tracers, depth_levels, across, lat_count = solute_fields.shape
    block = across * lat_count
    latitude = jnp.pi * (jnp.arange(lat_count).astype(jnp.float32) + 0.5) / lat_count - jnp.pi / 2
    rotation = CORIOLIS * jnp.sin(latitude)
    divisor = 1.0 + rotation * rotation
    zonal_flow_speed = (flow_vector[0] + rotation * flow_vector[1]) / divisor
    meridional_flow_speed = (flow_vector[1] - rotation * flow_vector[0]) / divisor
    top_level = shifted(jnp.stack([zonal_flow_speed[0], meridional_flow_speed[0]]), "sec", -1)
    east_below = jnp.concatenate([zonal_flow_speed[1:], top_level[:1]], axis=0)
    north_below = jnp.concatenate([meridional_flow_speed[1:], top_level[1:]], axis=0)
    shear = (zonal_flow_speed - east_below) ** 2 + (meridional_flow_speed - north_below) ** 2
    spreading_revised = 0.5 * vertical_spreading + 0.5 * shear / (1.0 + shear)
    thermal_bordered = with_halo(thermal_state, (("col", 1),), 1)
    thermal_carried = thermal_state + chemical_change(
        thermal_state,
        thermal_bordered[:, 2:],
        thermal_bordered[:, :-2],
        zonal_flow_speed,
        meridional_flow_speed,
    )
    padded_tracers = with_halo(solute_fields, (("col", 2),), 1)
    east_full, north_full, mixing_full = sent_together(
        (zonal_flow_speed, meridional_flow_speed, spreading_revised), "sec", 0, 1
    )
    water_sites = water_indicator.astype(jnp.float32)
    moved = solute_fields + water_sites * (
        chemical_change(
            solute_fields,
            padded_tracers[:, :, 2:],
            padded_tracers[:, :, :-2],
            east_full,
            north_full,
        )
        + column_mixing(solute_fields, mixing_full)
    )
    flat = moved.reshape(held_tracers, depth_levels, block)
    wet_flat = water_indicator.reshape(block)
    share = block // sections
    reacted = react(
        lax.all_to_all(flat, "sec", split_axis=2, concat_axis=0, tiled=True),
        linear_exchange_speeds,
        newton_preconditioner,
        absorption_speed,
    )
    merged = lax.all_to_all(reacted, "sec", split_axis=0, concat_axis=2, tiled=True)
    held_columns = section * share + jnp.arange(share, dtype=jnp.int32)
    warming_quantity = heating(reacted[0], sun_height(held_columns, lat_count))
    warmed_sites = lax.all_to_all(warming_quantity, "sec", split_axis=0, concat_axis=1, tiled=True)
    solute_revised = jnp.where(wet_flat[None, None, :] > 0, merged, flat).reshape(
        solute_fields.shape
    )
    thermal_revised = thermal_carried + CHLOROPHYLL_WARM * water_sites * warmed_sites.reshape(
        thermal_state.shape
    )
    return (
        thermal_revised,
        jnp.stack([zonal_flow_speed, meridional_flow_speed]),
        spreading_revised,
        solute_revised,
    )


def solution(mesh):
    placed = (
        P("sec", "col", None),
        P(None, "sec", "col", None),
        P("sec", "col", None),
        P("sec", None, "col", None),
        P(),
        P(),
        P(),
        P("col", None),
    )
    return jax.shard_map(
        on_device,
        mesh=mesh,
        in_specs=placed,
        out_specs=(
            P("sec", "col", None),
            P(None, "sec", "col", None),
            P("sec", "col", None),
            P("sec", None, "col", None),
        ),
        check_vma=False,
    )
```

profile of v0, /device:TPU:1, one launch (start us, length us, event | category | flops | bytes accessed | tf_op | source)
XLA Modules:
  0.0 313.5 jit_solution(1296617115949687864)
XLA Ops:
  7.3 1.0 fusion.33
  8.3 3.3 %collective-permute-start.4 = (f32[2,16,256]{2,1,0:T(8,128)S(1)}, f32[2,16,256]{2,1,0:T(8,128)S(1)}, u32[]{:S(2)}, u32[]{:S(2)}) collective-permute-start(f32[2,16,256]{2,1,0:T(8,128)S(1)} %pad_maximum_fusion.10), channel_id=1, source_target_pairs={{1,0},{2,1},{3,2},{4,3},{5,4},{6,5},{7,6},{8,7},{9,8},{10,9},{11,1... | collective-permute-start | bytes 98312 | tf_op jit(solution)/shard_map/ppermute | solution.py:21
  11.7 3.2 %collective-permute-done.4 = f32[2,16,256]{2,1,0:T(8,128)S(1)} collective-permute-done((f32[2,16,256]{2,1,0:T(8,128)S(1)}, f32[2,16,256]{2,1,0:T(8,128)S(1)}, u32[]{:S(2)}, u32[]{:S(2)}) %collective-permute-start.4) | collective-permute-done | bytes 32800 | tf_op jit(solution)/shard_map/ppermute | solution.py:21
  16.7 2.6 fusion.51
  19.3 3.6 %collective-permute-start.2 = (f32[2,128,1,256]{3,1,2,0:T(8,128)S(1)}, f32[2,128,1,256]{3,1,2,0:T(8,128)S(1)}, u32[]{:S(2)}, u32[]{:S(2)}) collective-permute-start(f32[2,128,1,256]{3,1,2,0:T(8,128)S(1)} %copy.34), channel_id=1, source_target_pairs={{16,0},{32,16},{48,32},{64,48},{80,64},{96,80},{112,96},{0,112},{1... | collective-permute-start | bytes 786440 | tf_op jit(solution)/shard_map/ppermute | solution.py:33
  23.0 8.3 %fusion.52 = (f32[2,128,16,255]{3,2,1,0:T(8,128)}, f32[2,128,16,255]{3,2,1,0:T(8,128)}) fusion(f32[2,128,16,256]{3,2,1,0:T(8,128)} %param.11), kind=kLoop, calls=%fused_computation.87 | loop fusion | bytes 16711680 | tf_op jit(solution)/shard_map/slice | solution.py:50
  31.3 2.0 fusion.53
  33.9 52.2 %all-gather.2.cloned.1.call-done = f32[128,48,256]{2,1,0:T(8,128)} async-done(((f32[8,48,256]{2,1,0:T(8,128)}), f32[128,48,256]{2,1,0:T(8,128)}) %all-gather.2.cloned.1.call-update) | async-done | bytes 6291472 | tf_op jit(solution)/shard_map/all_gather | solution.py:46
  86.0 2.0 slice_multiply_fusion
  88.0 6.9 %subtract_multiply_fusion = f32[2,127,16,256]{3,2,1,0:T(8,128)} fusion(f32[2,128,16,256]{3,2,1,0:T(8,128)} %param.11, f32[127,16,256]{2,1,0:T(8,128)S(1)} %slice_multiply_fusion), kind=kLoop, calls=%fused_computation.24 | loop fusion | flops 2080768 | bytes 14565376 | tf_op jit(solution)/shard_map/mul | solution.py:60
  95.0 2.6 fusion.50
  97.5 1.1 copy-done.2
  98.7 11.5 %multiply_add_fusion = f32[2,128,16,256]{3,2,1,0:T(8,128)} fusion(f32[2,128,16,256]{3,2,1,0:T(8,128)S(1)} %copy-done.2, f32[2,127,16,256]{3,2,1,0:T(8,128)} %subtract_multiply_fusion, f32[2,128,16,255]{3,2,1,0:T(8,128)} %get-tuple-element.9, f32[2,128,16,1]{3,2,1,0:T(8,128)} %get-tuple-element.11, f32[2,128,16,1]{3,2,1,0:T(8,128)S(1)} %get-tuple-element.10, ...), kind=kLoop, calls=%fused_computation.23 | loop fusion | flops 22020096 | bytes 25673728 | tf_op jit(solution)/shard_map/add | solution.py:130
  110.2 5.2 %copy.26 = f32[2,128,16,256]{1,0,3,2:T(2,128)} copy(f32[2,128,16,256]{3,2,1,0:T(8,128)} %multiply_add_fusion) | data formatting | bytes 8388608 | tf_op jit(solution)/shard_map/add | solution.py:130
  115.4 4.6 %all-to-all-start = ((f32[2,128,4096]{1,0,2:T(2,128)}), f32[2,128,4096]{1,0,2:T(2,128)}, u32[]{:S(2)}, u32[]{:S(2)}) async-start(f32[2,128,4096]{1,0,2:T(2,128)} %bitcast.75), calls=%async_computation | async-start | bytes 8388608 | tf_op jit(solution)/shard_map/all_to_all | solution.py:144
  120.1 53.3 %all-to-all-done = f32[2,128,4096]{1,0,2:T(2,128)} async-done(((f32[2,128,4096]{1,0,2:T(2,128)}), f32[2,128,4096]{1,0,2:T(2,128)}, u32[]{:S(2)}, u32[]{:S(2)}) %all-to-all-start) | async-done | bytes 4194336 | tf_op jit(solution)/shard_map/all_to_all | solution.py:144
  173.4 4.5 %copy.27 = f32[2,128,4096]{1,2,0:T(8,128)} copy(f32[2,128,4096]{1,0,2:T(2,128)} %all-to-all-done) | data formatting | bytes 8388608 | tf_op jit(solution)/shard_map/all_to_all | solution.py:144
  177.8 7.3 %copy.28 = f32[16,2,128,256]{3,1,0,2:T(2,128)} copy(f32[16,2,128,256]{2,3,0,1:T(8,128)} %bitcast.76) | data formatting | bytes 8388608 | tf_op jit(solution)/shard_map/all_to_all | solution.py:144
  185.2 6.0 %all_to_all.35 = f32[32,128,256]{2,0,1:T(8,128)} reshape(f32[16,2,128,256]{3,1,0,2:T(2,128)} %copy.28) | data formatting | bytes 8388608 | tf_op jit(solution)/shard_map/all_to_all | solution.py:144
  191.2 5.6 %fusion.40 = f32[128,256,32]{1,2,0:T(8,128)S(1)} fusion(f32[32,128,256]{2,0,1:T(8,128)} %all_to_all.35, f32[32,32]{1,0:T(8,128)S(1)} %copy-done), kind=kOutput, calls=%fused_computation.68 | convolution fusion | flops 402653184 | bytes 8392704 | tf_op jit(solution)/shard_map/ij,jlc->ilc/dot_general | solution.py:69
  196.8 5.4 %bitcast_subtract_fusion.2 = f32[32,128,256]{2,0,1:T(8,128)S(1)} fusion(f32[32,128,256]{2,0,1:T(8,128)S(1)} %copy-done.3, f32[128,256,32]{1,2,0:T(8,128)S(1)} %fusion.40, f32[32]{0:T(128)S(1)} %copy-done.10, f32[32,32]{1,0:T(8,128)S(1)} %copy-done.9), kind=kOutput, calls=%fused_computation.9 | convolution fusion | flops 411041792 | bytes 12587136 | tf_op jit(solution)/shard_map/ij,jlc->ilc/dot_general | solution.py:75
  202.2 4.0 %fusion.38 = f32[128,256,32]{1,2,0:T(8,128)S(1)} fusion(f32[32,128,256]{2,0,1:T(8,128)S(1)} %bitcast_subtract_fusion.2, f32[32,32]{1,0:T(8,128)S(1)} %copy-done), kind=kOutput, calls=%fused_computation.66 | convolution fusion | flops 402653184 | bytes 8392704 | tf_op jit(solution)/shard_map/ij,jlc->ilc/dot_general | solution.py:69
  206.2 5.6 %bitcast_subtract_fusion = f32[32,128,256]{2,0,1:T(8,128)S(1)} fusion(f32[32,128,256]{2,0,1:T(8,128)S(1)} %bitcast_subtract_fusion.2, f32[128,256,32]{1,2,0:T(8,128)S(1)} %fusion.38, f32[32,128,256]{2,0,1:T(8,128)S(1)} %copy-done.3, f32[32]{0:T(128)S(1)} %copy-done.10, f32[32,32]{1,0:T(8,128)S(1)} %copy-done.9), kind=kOutput, calls=%fused_computation.5 | convolution fusion | flops 411041792 | bytes 16781440 | tf_op jit(solution)/shard_map/ij,jlc->ilc/dot_general | solution.py:75
  211.8 2.0 copy-done.4
  214.9 13.4 %all-to-all-start.1 = ((f32[16,8,256]{2,1,0:T(8,128)}), f32[16,8,256]{2,1,0:T(8,128)S(1)}, u32[]{:S(2)}, u32[]{:S(2)}) async-start(f32[16,8,256]{2,1,0:T(8,128)} %fusion.30), calls=%async_computation.1 | async-start | bytes 262144 | tf_op jit(solution)/shard_map/all_to_all | solution.py:152
  228.3 6.6 %copy.30 = f32[32,128,256]{2,1,0:T(8,128)} copy(f32[32,128,256]{2,0,1:T(8,128)} %copy-done.4) | data formatting | bytes 8388608 | tf_op jit(solution)/shard_map/sub | solution.py:75
  234.9 1.0 all-to-all-done.1
  236.0 6.3 %all-to-all-start.2 = ((f32[32,128,256]{2,1,0:T(8,128)}), f32[32,128,256]{2,1,0:T(8,128)}, u32[]{:S(2)}, u32[]{:S(2)}) async-start(f32[32,128,256]{2,1,0:T(8,128)} %copy.30), calls=%async_computation.2 | async-start | bytes 8388608 | tf_op jit(solution)/shard_map/all_to_all | solution.py:149
  242.3 2.8 collective-permute-start
  246.1 48.3 %collective-permute-done = f32[8,1,256]{2,1,0:T(1,128)S(1)} collective-permute-done((f32[8,1,256]{2,1,0:T(1,128)S(1)}, f32[8,1,256]{2,1,0:T(1,128)S(1)}, u32[]{:S(2)}, u32[]{:S(2)}) %collective-permute-start) | collective-permute-done | bytes 8224 | tf_op jit(solution)/shard_map/ppermute | solution.py:33
  294.4 3.2 %collective-permute-done.1 = f32[8,1,256]{2,1,0:T(1,128)S(1)} collective-permute-done((f32[8,1,256]{2,1,0:T(1,128)S(1)}, f32[8,1,256]{2,1,0:T(1,128)S(1)}, u32[]{:S(2)}, u32[]{:S(2)}) %collective-permute-start.1) | collective-permute-done | bytes 8224 | tf_op jit(solution)/shard_map/ppermute | solution.py:31
  298.5 8.1 %bitcast_select_fusion = f32[2,128,16,256]{3,2,1,0:T(8,128)} fusion(f32[2,128,16,256]{3,2,1,0:T(8,128)} %multiply_add_fusion, f32[16,2,128,256]{3,2,1,0:T(8,128)} %bitcast.13, pred[16,256]{1,0:T(8,128)(4,1)S(1)} %broadcast_compare_fusion), kind=kLoop, calls=%fused_computation.4 | loop fusion | flops 1048576 | bytes 12587008 | tf_op jit(solution)/shard_map/jit(_where)/select_n | solution.py:153
  (59 shorter events, 5.6 us)
Async XLA Ops:
  7.2 184.0 %copy-start = (f32[32,32]{1,0:T(8,128)S(1)}, f32[32,32]{1,0:T(8,128)}, u32[]{:S(2)}) copy-start(f32[32,32]{1,0:T(8,128)} %param.12) | copy-start | bytes 12292
  7.2 15.8 %copy-start.8 = (s32[16,256]{1,0:T(8,128)S(1)}, s32[16,256]{1,0:T(8,128)}, u32[]{:S(2)}) copy-start(s32[16,256]{1,0:T(8,128)} %param.15) | copy-start | bytes 49156
  7.2 78.8 %all-gather.2.cloned.1.call-start = ((), (), s32[]{:S(2)}) async-start(), calls=%async_computation.3 | async-start | bytes 6684672 | tf_op jit(solution)/shard_map/all_gather | solution.py:46
  8.3 6.5 %collective-permute-start.4 = (f32[2,16,256]{2,1,0:T(8,128)S(1)}, f32[2,16,256]{2,1,0:T(8,128)S(1)}, u32[]{:S(2)}, u32[]{:S(2)}) collective-permute-start(f32[2,16,256]{2,1,0:T(8,128)S(1)} %pad_maximum_fusion.10), channel_id=1, source_target_pairs={{1,0},{2,1},{3,2},{4,3},{5,4},{6,5},{7,6},{8,7},{9,8},{10,9},{11,1... | collective-permute-start | bytes 98312 | tf_op jit(solution)/shard_map/ppermute | solution.py:21
  15.8 15.4 %copy-start.7 = (f32[8,16,256]{2,1,0:T(8,128)}, f32[8,16,256]{2,1,0:T(8,128)S(1)}, u32[]{:S(2)}) copy-start(f32[8,16,256]{2,1,0:T(8,128)S(1)} %divide_add_fusion) | copy-start | bytes 393220
  19.3 14.0 %collective-permute-start.2 = (f32[2,128,1,256]{3,1,2,0:T(8,128)S(1)}, f32[2,128,1,256]{3,1,2,0:T(8,128)S(1)}, u32[]{:S(2)}, u32[]{:S(2)}) collective-permute-start(f32[2,128,1,256]{3,1,2,0:T(8,128)S(1)} %copy.34), channel_id=1, source_target_pairs={{16,0},{32,16},{48,32},{64,48},{80,64},{96,80},{112,96},{0,112},{1... | collective-permute-start | bytes 786440 | tf_op jit(solution)/shard_map/ppermute | solution.py:33
  22.9 10.7 %collective-permute-start.3 = (f32[2,128,1,256]{3,1,2,0:T(8,128)S(1)}, f32[2,128,1,256]{3,1,2,0:T(8,128)S(1)}, u32[]{:S(2)}, u32[]{:S(2)}) collective-permute-start(f32[2,128,1,256]{3,1,2,0:T(8,128)S(1)} %copy.35), channel_id=1, source_target_pairs={{0,16},{16,32},{32,48},{48,64},{64,80},{80,96},{96,112},{112,0},{1... | collective-permute-start | bytes 786440 | tf_op jit(solution)/shard_map/ppermute | solution.py:31
  23.0 8.3 %copy-start.1 = (f32[2,128,16,256]{3,2,1,0:T(8,128)S(1)}, f32[2,128,16,256]{3,2,1,0:T(8,128)}, u32[]{:S(2)}) copy-start(f32[2,128,16,256]{3,2,1,0:T(8,128)} %param.11) | copy-start | bytes 12582916
  86.0 8.9 %slice-start = ((s8[6291456]{0:T(1024)(128)(4,1)}), s8[4194304]{0:T(1024)(128)(4,1)S(1)}, s32[]{:S(2)}) async-start(s8[6291456]{0:T(1024)(128)(4,1)} %bitcast.77), calls=%async_computation.4 | async-start | bytes 8388608
  88.0 6.9 %slice-start.1 = ((s8[6291456]{0:T(1024)(128)(4,1)}), s8[2097152]{0:T(1024)(128)(4,1)S(1)}, s32[]{:S(2)}) async-start(s8[6291456]{0:T(1024)(128)(4,1)} %bitcast.77), calls=%async_computation.5 | async-start | bytes 4194304
  95.0 3.7 %copy-start.2 = (f32[2,128,16,256]{3,2,1,0:T(8,128)S(1)}, f32[2,128,16,256]{3,2,1,0:T(8,128)}, u32[]{:S(2)}) copy-start(f32[2,128,16,256]{3,2,1,0:T(8,128)} %param.11) | copy-start | bytes 12582916
  115.4 58.0 %all-to-all-start = ((f32[2,128,4096]{1,0,2:T(2,128)}), f32[2,128,4096]{1,0,2:T(2,128)}, u32[]{:S(2)}, u32[]{:S(2)}) async-start(f32[2,128,4096]{1,0,2:T(2,128)} %bitcast.75), calls=%async_computation | async-start | bytes 8388608 | tf_op jit(solution)/shard_map/all_to_all | solution.py:144
  191.2 5.6 %copy-start.3 = (f32[32,128,256]{2,0,1:T(8,128)S(1)}, f32[32,128,256]{2,0,1:T(8,128)}, u32[]{:S(2)}) copy-start(f32[32,128,256]{2,0,1:T(8,128)} %all_to_all.35) | copy-start | bytes 12582916
  191.2 5.6 %copy-start.9 = (f32[32,32]{1,0:T(8,128)S(1)}, f32[32,32]{1,0:T(8,128)}, u32[]{:S(2)}) copy-start(f32[32,32]{1,0:T(8,128)} %param.13) | copy-start | bytes 12292
  191.2 5.6 %copy-start.10 = (f32[32]{0:T(128)S(1)}, f32[32]{0:T(128)}, u32[]{:S(2)}) copy-start(f32[32]{0:T(128)} %param.14) | copy-start | bytes 388
  211.8 2.0 copy-start.4
  214.9 21.1 %all-to-all-start.1 = ((f32[16,8,256]{2,1,0:T(8,128)}), f32[16,8,256]{2,1,0:T(8,128)S(1)}, u32[]{:S(2)}, u32[]{:S(2)}) async-start(f32[16,8,256]{2,1,0:T(8,128)} %fusion.30), calls=%async_computation.1 | async-start | bytes 262144 | tf_op jit(solution)/shard_map/all_to_all | solution.py:152
  234.9 7.4 %copy-start.5 = (f32[8,16,256]{2,1,0:T(8,128)S(1)}, f32[8,16,256]{2,1,0:T(8,128)}, u32[]{:S(2)}) copy-start(f32[8,16,256]{2,1,0:T(8,128)} %param.8) | copy-start | bytes 393220
  234.9 10.4 %copy-start.6 = (f32[2,8,16,256]{3,2,1,0:T(8,128)S(1)}, f32[2,8,16,256]{3,2,1,0:T(8,128)}, u32[]{:S(2)}) copy-start(f32[2,8,16,256]{3,2,1,0:T(8,128)} %param.9) | copy-start | bytes 786436
  236.0 62.5 %all-to-all-start.2 = ((f32[32,128,256]{2,1,0:T(8,128)}), f32[32,128,256]{2,1,0:T(8,128)}, u32[]{:S(2)}, u32[]{:S(2)}) async-start(f32[32,128,256]{2,1,0:T(8,128)} %copy.30), calls=%async_computation.2 | async-start | bytes 8388608 | tf_op jit(solution)/shard_map/all_to_all | solution.py:149
  242.3 52.1 %collective-permute-start = (f32[8,1,256]{2,1,0:T(1,128)S(1)}, f32[8,1,256]{2,1,0:T(1,128)S(1)}, u32[]{:S(2)}, u32[]{:S(2)}) collective-permute-start(f32[8,1,256]{2,1,0:T(1,128)S(1)} %get-tuple-element.17), channel_id=1, source_target_pairs={{16,0},{32,16},{48,32},{64,48},{80,64},{96,80},{112,96},{0,112},{1... | collective-permute-start | bytes 24584 | tf_op jit(solution)/shard_map/ppermute | solution.py:33
  245.1 52.5 %collective-permute-start.1 = (f32[8,1,256]{2,1,0:T(1,128)S(1)}, f32[8,1,256]{2,1,0:T(1,128)S(1)}, u32[]{:S(2)}, u32[]{:S(2)}) collective-permute-start(f32[8,1,256]{2,1,0:T(1,128)S(1)} %get-tuple-element.16), channel_id=1, source_target_pairs={{0,16},{16,32},{32,48},{48,64},{64,80},{80,96},{96,112},{112,0},{1... | collective-permute-start | bytes 24584 | tf_op jit(solution)/shard_map/ppermute | solution.py:31
Sparse Core Ops, SparseCore 0:
  16.8 69.1 all-gather.1
where the time goes:
time: 318 us; the launch traced here: 313 us
  waiting for transfers between devices  161 us (51%)
  local copies, waits for them, and re-layouts  49.1 us (15%)
  starting transfers between devices  34.2 us (11%)
  other arithmetic  34.1 us (11%)
  matrix products  20.5 us (6%)
  between operations  14.4 us (5%)
    all_to_all x1, waiting for transfers between devices, on_device(): lax.all_to_all(flat, 'sec', split_axis=2, concat_axis=0, tiled=True)  53.3 us
    all_gather x1, waiting for transfers between devices, sent_together(): lax.all_gather(both, axis, axis=dim, tiled=True)  52.2 us
    ppermute x2, waiting for transfers between devices, with_halo(): lax.ppermute(head, axis, [((i + 1) % count, i) for i in range(count)])  48.3 us
    all_to_all x3, local copies, waits for them, and re-layouts, on_device(): lax.all_to_all(flat, 'sec', split_axis=2, concat_axis=0, tiled=True)  17.8 us
    all_to_all x1, starting transfers between devices, on_device(): lax.all_to_all(warming_quantity, 'sec', split_axis=0, concat_axis=1, tile...  13.4 us
    add x1, other arithmetic, on_device(): solute_fields + water_sites * (chemical_change(solute_fields, padded_trac...  11.5 us
    dot_general x2, matrix products, react(): jnp.einsum('ij,jlc->ilc', newton_preconditioner, misfit, precision=lax.Pr...  11 us
    slice x4, local copies, waits for them, and re-layouts, chemical_change(): northern = jnp.concatenate([center[..., 1:], center[..., -1:]], axis=-1)  10.5 us
  transfers between devices with their start and end apart: 9, of which 6 were waited for; matrix products, arithmetic and copies ran while one was open for 7% of the time, Pallas kernels for 0%

commit v1 on v0

v1 whole, which is shorter than its diff:
```python
import jax
import jax.numpy as jnp
import numpy as np
from jax import lax
from jax.experimental import pallas as pl
from jax.experimental.pallas import tpu as pltpu
from jax.sharding import PartitionSpec as P

CORIOLIS = 0.8
MIXING = 0.1
VERTICAL_MIX = 0.3
WATER_ABSORB = 0.02
PIGMENT_ABSORB = 0.06
CHLOROPHYLL_WARM = 10.0

SECS = 16
COLS = 8
LEV = 8
LON = 16
TR = 32
LAT = 256
MESH = pl.DeviceIdType.MESH
F32 = jnp.float32
BF16 = jnp.bfloat16
HIGHEST = lax.Precision.HIGHEST


def saturating(value):
    return 1.0 - 1.0 / (1.0 + value * value)


def stacked_halves(top, bottom):
    both = jnp.concatenate([top, bottom], axis=0)
    high = both.astype(BF16)
    low = (both - high.astype(F32)).astype(BF16)
    return jnp.concatenate([high, low, high, low], axis=0)


def kernel(
    x, flow, kap, th, lin, pre, ab, wat, lat,
    th_o, vel_o, kap_o, sol_o,
    R, S, coef, lhs, flow_v, kap_v, th_v, lin_v, pre_v, ab_v, wat_v, lat_v,
    below_v, above_v, kabove_v, thh, vel_v, knext_v, pig, totals, thn_v,
    lsem, osem, small_s, small_r, hs, hr, fs, fr, vs, vr, bs, br, ps, ts, tr_,
):
    c = lax.axis_index("col")
    s = lax.axis_index("sec")
    left, right = (c + COLS - 1) % COLS, (c + 1) % COLS
    up, down = (s + SECS - 1) % SECS, (s + 1) % SECS

    loads = [
        pltpu.make_async_copy(a, b, lsem.at[i])
        for i, (a, b) in enumerate(
            [(flow, flow_v), (kap, kap_v), (th, th_v), (lin, lin_v), (pre, pre_v), (ab, ab_v), (wat, wat_v), (lat, lat_v)]
        )
    ]
    for copy in loads:
        copy.start()

    barrier = pltpu.get_barrier_semaphore()

    def greet(r, _):
        @pl.when(r > 0)
        def _():
            pl.semaphore_signal(barrier, inc=1, device_id=(c, s ^ r), device_id_type=MESH)

        pl.semaphore_signal(barrier, inc=1, device_id=(left, s ^ r), device_id_type=MESH)
        pl.semaphore_signal(barrier, inc=1, device_id=(right, s ^ r), device_id_type=MESH)
        return 0

    lax.fori_loop(0, SECS, greet, 0)
    pl.semaphore_wait(barrier, 3 * SECS - 1)

    def remote(src, dst, send, recv, to):
        return pltpu.make_async_remote_copy(
            src_ref=src, dst_ref=dst, send_sem=send, recv_sem=recv, device_id=to, device_id_type=MESH
        )

    smalls = [
        remote(flow.at[:, 0], below_v, small_s.at[0], small_r.at[0], (c, up)),
        remote(flow.at[:, LEV - 1], above_v, small_s.at[1], small_r.at[1], (c, down)),
        remote(kap.at[LEV - 1], kabove_v, small_s.at[2], small_r.at[2], (c, down)),
        remote(th.at[:, 0, :], thh.at[1, :, 0, :], small_s.at[3], small_r.at[3], (left, s)),
        remote(th.at[:, LON - 1, :], thh.at[0, :, 0, :], small_s.at[4], small_r.at[4], (right, s)),
    ]
    for copy in smalls:
        copy.start()

    def edges(r, _):
        d = s ^ r
        for t in range(2):
            remote(
                x.at[t, pl.ds(LEV * d, LEV), 0, :], R.at[pl.ds(1, LEV), LON + 1, 2 * s + t, :],
                hs, hr, (left, d),
            ).start()
            remote(
                x.at[t, pl.ds(LEV * d, LEV), LON - 1, :], R.at[pl.ds(1, LEV), 0, 2 * s + t, :],
                hs, hr, (right, d),
            ).start()
        return 0

    lax.fori_loop(0, SECS, edges, 0)

    def forward(i, _):
        k = lax.select(i == 1, LEV - 1, lax.select(i == 0, 0, i - 1))
        for t in range(2):
            pltpu.make_async_copy(
                x.at[t, LEV * s + k], R.at[k + 1, pl.ds(1, LON), 2 * s + t, :], fr.at[k]
            ).start()

        def peer(r, _):
            d = s ^ r
            for t in range(2):
                remote(
                    x.at[t, LEV * d + k], R.at[k + 1, pl.ds(1, LON), 2 * s + t, :],
                    fs.at[k], fr.at[k], (c, d),
                ).start()
            return 0

        lax.fori_loop(1, SECS, peer, 0)
        return 0

    lax.fori_loop(0, LEV, forward, 0)

    for copy in loads:
        copy.wait()
    for copy in smalls:
        copy.wait()

    rot = jnp.broadcast_to(lat_v[0:1, :], (LON, LAT))
    inv = 1.0 + rot * rot
    wet = wat_v[...].astype(F32)
    row = lax.broadcasted_iota(jnp.int32, (LON, LAT), 0)
    lane = lax.broadcasted_iota(jnp.int32, (LON, LAT), 1)

    def turned(u, v):
        return (u + rot * v) / inv, (v - rot * u) / inv

    below_ok = jnp.where(s == SECS - 1, 0.0, 1.0)
    above_ok = jnp.where(s == 0, 0.0, 1.0)
    east_a, north_a = turned(above_v[0], above_v[1])
    east_b, north_b = turned(below_v[0], below_v[1])
    east, north = turned(flow_v[0, 0], flow_v[1, 0])
    shear = (east_a - east) ** 2 + (north_a - north) ** 2
    k_up = (0.5 * kabove_v[...] + 0.5 * shear / (1.0 + shear)) * (VERTICAL_MIX * above_ok) * wet
    for k in range(LEV):
        vel_v[0, k] = east
        vel_v[1, k] = north
        if k < LEV - 1:
            east_n, north_n = turned(flow_v[0, k + 1], flow_v[1, k + 1])
        else:
            east_n, north_n = east_b * below_ok, north_b * below_ok
        shear = (east - east_n) ** 2 + (north - north_n) ** 2
        knext = 0.5 * kap_v[k] + 0.5 * shear / (1.0 + shear)
        knext_v[k] = knext
        k_down = knext * VERTICAL_MIX * wet
        if k == LEV - 1:
            k_down = k_down * below_ok
        coef[k, 0] = (1.0 - 4.0 * MIXING * wet) - k_down - k_up
        coef[k, 1] = (MIXING - MIXING * east) * wet
        coef[k, 2] = (MIXING + MIXING * east) * wet
        coef[k, 3] = (MIXING - MIXING * north) * wet
        coef[k, 4] = (MIXING + MIXING * north) * wet
        coef[k, 5] = k_down
        coef[k, 6] = k_up
        f = th_v[k]
        f_e = jnp.where(row == LON - 1, jnp.broadcast_to(thh[1, k, 0:1, :], (LON, LAT)), pltpu.roll(f, LON - 1, 0))
        f_w = jnp.where(row == 0, jnp.broadcast_to(thh[0, k, 0:1, :], (LON, LAT)), pltpu.roll(f, 1, 0))
        f_n = jnp.where(lane == LAT - 1, f, pltpu.roll(f, LAT - 1, 1))
        f_s = jnp.where(lane == 0, f, pltpu.roll(f, 1, 1))
        thn_v[k] = (
            f + MIXING * (f_e + f_w + f_n + f_s - 4.0 * f)
            - MIXING * (east * (f_e - f_w) + north * (f_n - f_s))
        )
        east, north, k_up = east_n, north_n, k_down
    outs = [pltpu.make_async_copy(vel_v, vel_o, osem.at[0]), pltpu.make_async_copy(knext_v, kap_o, osem.at[1])]
    for copy in outs:
        copy.start()

    inner = jnp.dot(pre_v[...], lin_v[...], precision=HIGHEST, preferred_element_type=F32)
    scaled = pre_v[...] * ab_v[...]
    at = lax.broadcasted_iota(jnp.int32, (TR, LAT), 1)
    which = lax.broadcasted_iota(jnp.int32, (TR, LAT), 0)
    pick_m = (at % (2 * TR) == which).astype(F32)
    pick_s = (at % (2 * TR) == which + TR).astype(F32)
    first = jnp.dot(inner, pick_m, precision=HIGHEST, preferred_element_type=F32) - jnp.dot(
        scaled, pick_s, precision=HIGHEST, preferred_element_type=F32
    )
    second = -jnp.dot(pre_v[...], first, precision=HIGHEST, preferred_element_type=F32)
    for i, rows in enumerate((first, second)):
        high = rows.astype(BF16)
        low = rows - high.astype(F32)
        lhs[pl.ds(TR * i, TR), :] = jnp.where(at < 4 * TR, high.astype(F32), low).astype(BF16)

    def all_of(k, sem):
        pltpu.make_async_copy(R.at[k + 1, pl.ds(1, LON)], R.at[k + 1, pl.ds(1, LON)], sem).wait()

    all_of(0, fr.at[0])
    all_of(LEV - 1, fr.at[LEV - 1])
    verticals = [
        remote(R.at[1, pl.ds(1, LON)], R.at[LEV + 1, pl.ds(1, LON)], vs.at[0], vr.at[0], (c, up)),
        remote(R.at[LEV, pl.ds(1, LON)], R.at[0, pl.ds(1, LON)], vs.at[1], vr.at[1], (c, down)),
    ]
    for copy in verticals:
        copy.start()
    edge = R.at[pl.ds(1, LEV), pl.ds(0, 2)]
    pltpu.make_async_copy(edge, edge, hr).wait()
    all_of(1, fr.at[1])

    tlane = lax.broadcasted_iota(jnp.int32, (TR, LAT), 1)

    def level(i, _):
        k = lax.select(i == LEV - 1, LEV - 1, lax.select(i == LEV - 2, 0, i + 1))

        @pl.when(i < LEV - 3)
        def _():
            all_of(i + 2, fr.at[i + 2])

        @pl.when(i == LEV - 2)
        def _():
            verticals[1].wait_recv()

        @pl.when(i == LEV - 1)
        def _():
            verticals[0].wait_recv()

        def column(j, _):
            def row_of(n):
                return jnp.broadcast_to(coef[k, n, pl.ds(j, 1), :], (TR, LAT))

            center = R[k + 1, j + 1]
            moved = row_of(0) * center
            moved += row_of(1) * R[k + 1, j + 2]
            moved += row_of(2) * R[k + 1, j]
            moved += row_of(3) * jnp.where(tlane == LAT - 1, center, pltpu.roll(center, LAT - 1, 1))
            moved += row_of(4) * jnp.where(tlane == 0, center, pltpu.roll(center, 1, 1))
            moved += row_of(5) * R[k + 2, j + 1]
            moved += row_of(6) * R[k, j + 1]
            y = jnp.dot(lhs[...], stacked_halves(moved, saturating(moved)), preferred_element_type=F32)
            current = moved + y[:TR]
            base = current + y[TR:]
            y = jnp.dot(lhs[:TR, :], stacked_halves(current, saturating(current)), preferred_element_type=F32)
            wet_row = jnp.broadcast_to(wat_v[pl.ds(j, 1), :], (TR, LAT))
            S[k, j] = jnp.where(wet_row > 0, base + y, moved)
            return 0

        lax.fori_loop(0, LON, column, 0, unroll=2)

        pltpu.make_async_copy(S.at[k, :, 0, :], pig.at[k], ps).start()
        for t in range(2):
            pltpu.make_async_copy(S.at[k, :, 2 * s + t, :], sol_o.at[t, LEV * s + k], br.at[k]).start()

        def peer(r, _):
            d = s ^ r
            for t in range(2):
                remote(
                    S.at[k, :, 2 * d + t, :], sol_o.at[t, LEV * s + k], bs.at[k], br.at[k], (c, d)
                ).start()
            return 0

        lax.fori_loop(1, SECS, peer, 0)
        return 0

    lax.fori_loop(0, LEV, level, 0)

    pltpu.make_async_copy(pig, pig, ps).wait()
    total = jnp.zeros((LON, LAT), F32)
    for k in range(LEV):
        total += WATER_ABSORB + PIGMENT_ABSORB * saturating(pig[k])
    totals[s] = total

    def tell(r, _):
        remote(totals.at[s], totals.at[s], ts, tr_, (c, s ^ r)).start()
        return 0

    lax.fori_loop(1, SECS, tell, 0)
    others = totals.at[pl.ds(0, SECS - 1)]
    pltpu.make_async_copy(others, others, tr_).wait()
    depth = jnp.zeros((LON, LAT), F32)
    for d in range(SECS):
        depth += totals[d] * jnp.where(d < s, 1.0, 0.0)
    light = CHLOROPHYLL_WARM * jnp.broadcast_to(lat_v[1:2, :], (LON, LAT)) * wet
    before = jnp.exp(-depth)
    for k in range(LEV):
        depth = depth + (WATER_ABSORB + PIGMENT_ABSORB * saturating(pig[k]))
        after = jnp.exp(-depth)
        thn_v[k] = thn_v[k] + light * (before - after)
        before = after
    outs.append(pltpu.make_async_copy(thn_v, th_o, osem.at[2]))
    outs[-1].start()

    pltpu.make_async_copy(others, others, ts).wait()
    pltpu.make_async_copy(edge, edge, hs).wait()
    for copy in verticals:
        copy.wait_send()
    sent = R.at[1, pl.ds(1, LON - 1)]

    def finish(k, _):
        pltpu.make_async_copy(sent, sent, fs.at[k]).wait()
        pltpu.make_async_copy(sent, sent, bs.at[k]).wait()
        back = sol_o.at[0, pl.ds(0, 2 * SECS)]
        pltpu.make_async_copy(back, back, br.at[k]).wait()
        return 0

    lax.fori_loop(0, LEV, finish, 0)
    for copy in outs:
        copy.wait()


def on_device(thermal, flow, spreading, solute, lin, pre, ab, water):
    index = (np.arange(LAT, dtype=np.float64) + 0.5) * np.pi / LAT - np.pi / 2
    table = np.zeros((8, LAT), np.float32)
    table[0] = CORIOLIS * np.sin(index)
    table[1] = np.cos(index)
    hbm = pl.BlockSpec(memory_space=pl.ANY)
    dma = pltpu.SemaphoreType.DMA
    return pl.pallas_call(
        kernel,
        out_shape=(
            jax.ShapeDtypeStruct(thermal.shape, F32),
            jax.ShapeDtypeStruct(flow.shape, F32),
            jax.ShapeDtypeStruct(spreading.shape, F32),
            jax.ShapeDtypeStruct(solute.shape, F32),
        ),
        in_specs=[hbm] * 9,
        out_specs=(hbm,) * 4,
        scratch_shapes=[
            pltpu.VMEM((LEV + 2, LON + 2, TR, LAT), F32),
            pltpu.VMEM((LEV, LON, TR, LAT), F32),
            pltpu.VMEM((LEV, 7, LON, LAT), F32),
            pltpu.VMEM((2 * TR, LAT), BF16),
            pltpu.VMEM((2, LEV, LON, LAT), F32),
            pltpu.VMEM((LEV, LON, LAT), F32),
            pltpu.VMEM((LEV, LON, LAT), F32),
            pltpu.VMEM((TR, TR), F32),
            pltpu.VMEM((TR, TR), F32),
            pltpu.VMEM((1, TR), F32),
            pltpu.VMEM((LON, LAT), jnp.int32),
            pltpu.VMEM((8, LAT), F32),
            pltpu.VMEM((2, LON, LAT), F32),
            pltpu.VMEM((2, LON, LAT), F32),
            pltpu.VMEM((LON, LAT), F32),
            pltpu.VMEM((2, LEV, 8, LAT), F32),
            pltpu.VMEM((2, LEV, LON, LAT), F32),
            pltpu.VMEM((LEV, LON, LAT), F32),
            pltpu.VMEM((LEV, LON, LAT), F32),
            pltpu.VMEM((SECS, LON, LAT), F32),
            pltpu.VMEM((LEV, LON, LAT), F32),
            dma((8,)), dma((3,)), dma((5,)), dma((5,)),
            dma, dma, dma((LEV,)), dma((LEV,)), dma((2,)), dma((2,)), dma((LEV,)), dma((LEV,)),
            dma, dma, dma,
        ],
        compiler_params=pltpu.CompilerParams(
            collective_id=0, has_side_effects=True, vmem_limit_bytes=56 << 20
        ),
        name="ocean_step",
    )(solute, flow, spreading, thermal, lin, pre, ab.reshape(1, TR), water, jnp.asarray(table))


def solution(mesh):
    placed = (
        P("sec", "col", None),
        P(None, "sec", "col", None),
        P("sec", "col", None),
        P("sec", None, "col", None),
        P(),
        P(),
        P(),
        P("col", None),
    )
    return jax.shard_map(
        on_device,
        mesh=mesh,
        in_specs=placed,
        out_specs=placed[:1] + placed[1:4],
        check_vma=False,
    )
```

time: 318 us -> 184 us (0.58)
  the two profiles are of different devices: /device:TPU:1 before, /device:TPU:9 now
where the time goes in v1:
time: 184 us
  Pallas kernels  173 us (94%)
  local copies, waits for them, and re-layouts  9.44 us (5%)
    pallas_call x1, Pallas kernels, on_device(): pl.pallas_call(kernel, out_shape=(jax.ShapeDtypeStruct(thermal.shape, F32...  173 us
    unnamed x4, local copies, waits for them, and re-layouts  9.44 us

profile of v1, /device:TPU:9, one launch (start us, length us, event | category | flops | bytes accessed | tf_op | source)
XLA Modules:
  0.0 183.5 jit_solution(10282459472706155966)
XLA Ops:
  0.6 173.4 %ocean_step.1 = (f32[8,16,256]{2,1,0:T(8,128)}, f32[2,8,16,256]{3,2,1,0:T(8,128)}, f32[8,16,256]{2,1,0:T(8,128)}, f32[2,128,16,256]{3,2,1,0:T(8,128)}) custom-call(f32[2,128,16,256]{3,2,1,0:T(8,128)} %x.1, f32[2,8,16,256]{3,2,1,0:T(8,128)} %flow.1, f32[8,16,256]{2,1,0:T(8,128)} %kap.1, f32[8,16,256]{2,1,0:T(8,128)} %th.1, f32[32,32]{1,0:T(8,128)} %lin.1, ...), custom_call_target="tpu_custom_call" | custom-call | tf_op jit(solution)/shard_map/ocean_step/pallas_call | solution.py:317
  174.1 1.6 copy.17
  175.6 1.7 copy.18
  177.3 1.6 copy.19
  178.9 4.6 %copy.20 = f32[2,128,16,256]{3,2,1,0:T(8,128)} copy(f32[2,128,16,256]{3,2,1,0:T(8,128)} %get-tuple-element.11) | data formatting | bytes 8388608

commit v2 on v1

--- a/solution.py
+++ b/solution.py
@@ -19,6 +19,7 @@
 LON = 16
 TR = 32
 LAT = 256
+AHEAD = 4
 MESH = pl.DeviceIdType.MESH
 F32 = jnp.float32
 BF16 = jnp.bfloat16
@@ -60,16 +61,13 @@
     barrier = pltpu.get_barrier_semaphore()
 
     def greet(r, _):
-        @pl.when(r > 0)
-        def _():
-            pl.semaphore_signal(barrier, inc=1, device_id=(c, s ^ r), device_id_type=MESH)
-
-        pl.semaphore_signal(barrier, inc=1, device_id=(left, s ^ r), device_id_type=MESH)
-        pl.semaphore_signal(barrier, inc=1, device_id=(right, s ^ r), device_id_type=MESH)
-        return 0
-
-    lax.fori_loop(0, SECS, greet, 0)
-    pl.semaphore_wait(barrier, 3 * SECS - 1)
+        pl.semaphore_signal(barrier, inc=1, device_id=(c, s ^ r), device_id_type=MESH)
+        return 0
+
+    lax.fori_loop(1, SECS, greet, 0)
+    pl.semaphore_signal(barrier, inc=1, device_id=(left, s), device_id_type=MESH)
+    pl.semaphore_signal(barrier, inc=1, device_id=(right, s), device_id_type=MESH)
+    pl.semaphore_wait(barrier, SECS + 1)
 
     def remote(src, dst, send, recv, to):
         return pltpu.make_async_remote_copy(
@@ -86,21 +84,6 @@
     for copy in smalls:
         copy.start()
 
-    def edges(r, _):
-        d = s ^ r
-        for t in range(2):
-            remote(
-                x.at[t, pl.ds(LEV * d, LEV), 0, :], R.at[pl.ds(1, LEV), LON + 1, 2 * s + t, :],
-                hs, hr, (left, d),
-            ).start()
-            remote(
-                x.at[t, pl.ds(LEV * d, LEV), LON - 1, :], R.at[pl.ds(1, LEV), 0, 2 * s + t, :],
-                hs, hr, (right, d),
-            ).start()
-        return 0
-
-    lax.fori_loop(0, SECS, edges, 0)
-
     def forward(i, _):
         k = lax.select(i == 1, LEV - 1, lax.select(i == 0, 0, i - 1))
         for t in range(2):
@@ -120,7 +103,7 @@
         lax.fori_loop(1, SECS, peer, 0)
         return 0
 
-    lax.fori_loop(0, LEV, forward, 0)
+    lax.fori_loop(0, AHEAD, forward, 0)
 
     for copy in loads:
         copy.wait()
@@ -195,26 +178,45 @@
     def all_of(k, sem):
         pltpu.make_async_copy(R.at[k + 1, pl.ds(1, LON)], R.at[k + 1, pl.ds(1, LON)], sem).wait()
 
-    all_of(0, fr.at[0])
-    all_of(LEV - 1, fr.at[LEV - 1])
     verticals = [
         remote(R.at[1, pl.ds(1, LON)], R.at[LEV + 1, pl.ds(1, LON)], vs.at[0], vr.at[0], (c, up)),
         remote(R.at[LEV, pl.ds(1, LON)], R.at[0, pl.ds(1, LON)], vs.at[1], vr.at[1], (c, down)),
     ]
-    for copy in verticals:
-        copy.start()
+
+    def arrived(i, _):
+        k = lax.select(i == 1, LEV - 1, lax.select(i == 0, 0, i - 1))
+        all_of(k, fr.at[k])
+        remote(R.at[k + 1, 1], R.at[k + 1, LON + 1], hs, hr.at[k], (left, s)).start()
+        remote(R.at[k + 1, LON], R.at[k + 1, 0], hs, hr.at[k], (right, s)).start()
+
+        @pl.when(i == 0)
+        def _():
+            verticals[0].start()
+
+        @pl.when(i == 1)
+        def _():
+            verticals[1].start()
+
+        @pl.when(i < LEV - AHEAD)
+        def _():
+            forward(i + AHEAD, 0)
+
+        return 0
+
     edge = R.at[pl.ds(1, LEV), pl.ds(0, 2)]
-    pltpu.make_async_copy(edge, edge, hr).wait()
-    all_of(1, fr.at[1])
+    lax.fori_loop(0, 4, arrived, 0)
 
     tlane = lax.broadcasted_iota(jnp.int32, (TR, LAT), 1)
 
     def level(i, _):
         k = lax.select(i == LEV - 1, LEV - 1, lax.select(i == LEV - 2, 0, i + 1))
 
-        @pl.when(i < LEV - 3)
-        def _():
-            all_of(i + 2, fr.at[i + 2])
+        @pl.when(i < LEV - 4)
+        def _():
+            arrived(i + 4, 0)
+
+        both = R.at[k + 1, pl.ds(0, 2)]
+        pltpu.make_async_copy(both, both, hr.at[k]).wait()
 
         @pl.when(i == LEV - 2)
         def _():
@@ -307,23 +309,32 @@
         copy.wait()
 
 
+def settle(*refs):
+    given, made, sem = refs[:4], refs[4:8], refs[8]
+    copies = [pltpu.make_async_copy(a, b, sem.at[i]) for i, (a, b) in enumerate(zip(given, made))]
+    for copy in copies:
+        copy.start()
+    for copy in copies:
+        copy.wait()
+
+
 def on_device(thermal, flow, spreading, solute, lin, pre, ab, water):
     index = (np.arange(LAT, dtype=np.float64) + 0.5) * np.pi / LAT - np.pi / 2
     table = np.zeros((8, LAT), np.float32)
     table[0] = CORIOLIS * np.sin(index)
     table[1] = np.cos(index)
-    hbm = pl.BlockSpec(memory_space=pl.ANY)
+    hbm = pl.BlockSpec(memory_space=pltpu.HBM)
     dma = pltpu.SemaphoreType.DMA
-    return pl.pallas_call(
+    shapes = tuple(
+        jax.ShapeDtypeStruct(a.shape, F32) for a in (thermal, flow, spreading, solute)
+    )
+    vmem = pl.BlockSpec(memory_space=pltpu.VMEM)
+    given = (solute, flow, spreading, thermal, lin, pre, ab.reshape(1, TR), water, jnp.asarray(table))
+    results = pl.pallas_call(
         kernel,
-        out_shape=(
-            jax.ShapeDtypeStruct(thermal.shape, F32),
-            jax.ShapeDtypeStruct(flow.shape, F32),
-            jax.ShapeDtypeStruct(spreading.shape, F32),
-            jax.ShapeDtypeStruct(solute.shape, F32),
-        ),
+        out_shape=shapes,
         in_specs=[hbm] * 9,
-        out_specs=(hbm,) * 4,
+        out_specs=(vmem,) * 4,
         scratch_shapes=[
             pltpu.VMEM((LEV + 2, LON + 2, TR, LAT), F32),
             pltpu.VMEM((LEV, LON, TR, LAT), F32),
@@ -347,14 +358,23 @@
             pltpu.VMEM((SECS, LON, LAT), F32),
             pltpu.VMEM((LEV, LON, LAT), F32),
             dma((8,)), dma((3,)), dma((5,)), dma((5,)),
-            dma, dma, dma((LEV,)), dma((LEV,)), dma((2,)), dma((2,)), dma((LEV,)), dma((LEV,)),
+            dma, dma((LEV,)), dma((LEV,)), dma((LEV,)), dma((2,)), dma((2,)), dma((LEV,)), dma((LEV,)),
             dma, dma, dma,
         ],
         compiler_params=pltpu.CompilerParams(
-            collective_id=0, has_side_effects=True, vmem_limit_bytes=56 << 20
+            collective_id=0, has_side_effects=True, vmem_limit_bytes=28 << 20
         ),
         name="ocean_step",
-    )(solute, flow, spreading, thermal, lin, pre, ab.reshape(1, TR), water, jnp.asarray(table))
+    )(*(pltpu.with_memory_space_constraint(a, pltpu.HBM) for a in given))
+    return pl.pallas_call(
+        settle,
+        out_shape=shapes,
+        in_specs=[vmem] * 4,
+        out_specs=(hbm,) * 4,
+        scratch_shapes=[dma((4,))],
+        compiler_params=pltpu.CompilerParams(vmem_limit_bytes=16 << 20),
+        name="settle",
+    )(*results)
 
 
 def solution(mesh):

time: 184 us -> 126 us (0.68)
  the two profiles are of different devices: /device:TPU:9 before, /device:TPU:1 now
where the time goes in v2:
time: 126 us
  Pallas kernels  125 us (99%)
    pallas_call x1, Pallas kernels, on_device(): pl.pallas_call(kernel, out_shape=shapes, in_specs=[hbm] * 9, out_specs=(v...  123 us

profile of v2, /device:TPU:1, one launch (start us, length us, event | category | flops | bytes accessed | tf_op | source)
XLA Modules:
  0.0 125.8 jit_solution(14615403156577390546)
XLA Ops:
  0.6 122.9 %ocean_step.1 = (f32[8,16,256]{2,1,0:T(8,128)S(1)}, f32[2,8,16,256]{3,2,1,0:T(8,128)S(1)}, f32[8,16,256]{2,1,0:T(8,128)S(1)}, f32[2,128,16,256]{3,2,1,0:T(8,128)S(1)}) custom-call(f32[2,128,16,256]{3,2,1,0:T(8,128)} %x.1, f32[2,8,16,256]{3,2,1,0:T(8,128)} %flow.1, f32[8,16,256]{2,1,0:T(8,128)} %kap.1, f32[8,16,256]{2,1,0:T(8,128)} %th.1, f32[32,32]{1,0:T(8,128)} %lin.1, ...), custom_call_target="tpu_custom_call" | custom-call | tf_op jit(solution)/shard_map/ocean_step/pallas_call | solution.py:333
  123.6 2.2 %settle.1 = (f32[8,16,256]{2,1,0:T(8,128)}, f32[2,8,16,256]{3,2,1,0:T(8,128)}, f32[8,16,256]{2,1,0:T(8,128)}, f32[2,128,16,256]{3,2,1,0:T(8,128)}) custom-call(f32[8,16,256]{2,1,0:T(8,128)S(1)} %get-tuple-element.8.refs_0_, f32[2,8,16,256]{3,2,1,0:T(8,128)S(1)} %get-tuple-element.9.refs_1_, f32[8,16,256]{2,1,0:T(8,128)S(1)} %get-tuple-element.10.refs_2_, ...), custom_call_target="tpu_custom_call" | custom-call | tf_op jit(solution)/shard_map/settle/pallas_call | solution.py:369

commit v3 on v2

--- a/solution.py
+++ b/solution.py
@@ -20,6 +20,10 @@
 TR = 32
 LAT = 256
 AHEAD = 4
+KEPT = 12
+BITS = 5
+HALF = 128
+PIECES = LON * LAT // HALF
 MESH = pl.DeviceIdType.MESH
 F32 = jnp.float32
 BF16 = jnp.bfloat16
@@ -37,12 +41,16 @@
     return jnp.concatenate([high, low, high, low], axis=0)
 
 
+def along(piece, index):
+    return jnp.take_along_axis(piece, index, axis=1)
+
+
 def kernel(
     x, flow, kap, th, lin, pre, ab, wat, lat,
     th_o, vel_o, kap_o, sol_o,
-    R, S, coef, lhs, flow_v, kap_v, th_v, lin_v, pre_v, ab_v, wat_v, lat_v,
-    below_v, above_v, kabove_v, thh, vel_v, knext_v, pig, totals, thn_v,
-    lsem, osem, small_s, small_r, hs, hr, fs, fr, vs, vr, bs, br, ps, ts, tr_,
+    R, S, C, D, comes, goes, gather, scatter, coef, lhs, flow_v, kap_v, th_v, lin_v, pre_v, ab_v, wat_v, lat_v,
+    below_v, above_v, kabove_v, thh, vel_v, knext_v, pig, totals, thn_v, scr_v,
+    lsem, osem, small_s, small_r, hs, hr, fs, fr, vs, vr, bs, br, ts, tr_, xs,
 ):
     c = lax.axis_index("col")
     s = lax.axis_index("sec")
@@ -104,6 +112,9 @@
         return 0
 
     lax.fori_loop(0, AHEAD, forward, 0)
+
+    original = pltpu.make_async_copy(x, sol_o, xs)
+    original.start()
 
     for copy in loads:
         copy.wait()
@@ -175,6 +186,55 @@
         low = rows - high.astype(F32)
         lhs[pl.ds(TR * i, TR), :] = jnp.where(at < 4 * TR, high.astype(F32), low).astype(BF16)
 
+    lane8 = lax.broadcasted_iota(jnp.int32, (8, HALF), 1)
+    wide = lax.broadcasted_iota(jnp.int32, (LAT, LAT), 0)
+    wide_t = lax.broadcasted_iota(jnp.int32, (LAT, LAT), 1)
+    same = wide // HALF == wide_t // HALF
+    ahead_of = jnp.where(same & (wide < wide_t), 1.0, 0.0).astype(BF16)
+    beside = jnp.where(same, 1.0, 0.0).astype(BF16)
+    left_of = jnp.where(wide // HALF < wide_t // HALF, 1.0, 0.0).astype(BF16)
+    row_t = lax.broadcasted_iota(jnp.int32, (LON, LON), 1)
+    rows_before = jnp.where(lax.broadcasted_iota(jnp.int32, (LON, LON), 0) > row_t, 1.0, 0.0).astype(BF16)
+    wet_b = wet.astype(BF16)
+    rank = jnp.dot(wet_b, ahead_of, preferred_element_type=F32)
+    before = jnp.dot(rows_before, wet_b, preferred_element_type=F32)
+    before = jnp.dot(before.astype(BF16), jnp.ones((LAT, LAT), BF16), preferred_element_type=F32)
+    before = before + jnp.dot(wet_b, left_of, preferred_element_type=F32)
+    tables = [rank, before, jnp.dot(wet_b, beside, preferred_element_type=F32), wet]
+    for i, table in enumerate(tables):
+        scr_v[i] = table.astype(jnp.int32)
+
+    def piece_of(i, v):
+        part = scr_v[i, v // 2 : v // 2 + 1, (v % 2) * HALF : (v % 2 + 1) * HALF]
+        return jnp.broadcast_to(part, (8, HALF))
+
+    shift = []
+    for v in range(PIECES):
+        ranks, start, count, is_wet = (piece_of(i, v) for i in range(4))
+        scatter[v] = (start + ranks) & (HALF - 1)
+        lanes, moves = lane8, jnp.where(is_wet > 0, lane8 - ranks, 0)
+        for bit in range(7):
+            by = 1 << bit
+            inside = lane8 < HALF - by
+            next_m = jnp.where(inside, pltpu.roll(moves, HALF - by, 1), 0)
+            enters = (next_m & by) > 0
+            lanes = jnp.where(enters, pltpu.roll(lanes, HALF - by, 1), lanes)
+            moves = jnp.where(enters, next_m, jnp.where((moves & by) > 0, 0, moves))
+        turn = (lane8 - start) & (HALF - 1)
+        gather[v] = along(lanes, turn)
+        shift.append(jnp.where(turn < count, v - ((start + turn) >> 7), 0))
+    for bit in range(BITS):
+        far = 1 << bit
+        for v in range(PIECES):
+            leaves = (shift[v] >> bit) & 1
+            goes[bit * PIECES + v] = leaves
+            if v + far < PIECES:
+                enters = (shift[v + far] >> bit) & 1
+                comes[bit * PIECES + v] = enters
+                shift[v] = jnp.where(enters > 0, shift[v + far], jnp.where(leaves > 0, 0, shift[v]))
+            else:
+                shift[v] = jnp.where(leaves > 0, 0, shift[v])
+
     def all_of(k, sem):
         pltpu.make_async_copy(R.at[k + 1, pl.ds(1, LON)], R.at[k + 1, pl.ds(1, LON)], sem).wait()
 
@@ -210,10 +270,6 @@
 
     def level(i, _):
         k = lax.select(i == LEV - 1, LEV - 1, lax.select(i == LEV - 2, 0, i + 1))
-
-        @pl.when(i < LEV - 4)
-        def _():
-            arrived(i + 4, 0)
 
         both = R.at[k + 1, pl.ds(0, 2)]
         pltpu.make_async_copy(both, both, hr.at[k]).wait()
@@ -243,29 +299,49 @@
             base = current + y[TR:]
             y = jnp.dot(lhs[:TR, :], stacked_halves(current, saturating(current)), preferred_element_type=F32)
             wet_row = jnp.broadcast_to(wat_v[pl.ds(j, 1), :], (TR, LAT))
-            S[k, j] = jnp.where(wet_row > 0, base + y, moved)
+            reacted = jnp.where(wet_row > 0, base + y, moved)
+            S[j] = reacted
+            pig[k, pl.ds(j, 1), :] = reacted[0:1]
             return 0
 
         lax.fori_loop(0, LON, column, 0, unroll=2)
 
-        pltpu.make_async_copy(S.at[k, :, 0, :], pig.at[k], ps).start()
+        @pl.when(i < LEV - 4)
+        def _():
+            arrived(i + 4, 0)
+
+        def pack(g, _):
+            pieces = [
+                along(S[v // 2, pl.ds(8 * g, 8), (v % 2) * HALF : (v % 2 + 1) * HALF], gather[v])
+                for v in range(PIECES)
+            ]
+            for bit in range(BITS):
+                far = 1 << bit
+                for v in range(PIECES - far):
+                    pieces[v] = jnp.where(comes[bit * PIECES + v] > 0, pieces[v + far], pieces[v])
+            for v in range(2 * KEPT):
+                C[k, v // 2, pl.ds(8 * g, 8), (v % 2) * HALF : (v % 2 + 1) * HALF] = pieces[v]
+            return 0
+
+        lax.fori_loop(0, TR // 8, pack, 0)
+
         for t in range(2):
-            pltpu.make_async_copy(S.at[k, :, 2 * s + t, :], sol_o.at[t, LEV * s + k], br.at[k]).start()
+            pltpu.make_async_copy(C.at[k, :, 2 * s + t, :], D.at[k, t, :, s, :], br.at[k]).start()
 
         def peer(r, _):
             d = s ^ r
             for t in range(2):
                 remote(
-                    S.at[k, :, 2 * d + t, :], sol_o.at[t, LEV * s + k], bs.at[k], br.at[k], (c, d)
+                    C.at[k, :, 2 * d + t, :], D.at[k, t, :, s, :], bs.at[k], br.at[k], (c, d)
                 ).start()
             return 0
 
         lax.fori_loop(1, SECS, peer, 0)
+
         return 0
 
     lax.fori_loop(0, LEV, level, 0)
 
-    pltpu.make_async_copy(pig, pig, ps).wait()
     total = jnp.zeros((LON, LAT), F32)
     for k in range(LEV):
         total += WATER_ABSORB + PIGMENT_ABSORB * saturating(pig[k])
@@ -297,11 +373,43 @@
         copy.wait_send()
     sent = R.at[1, pl.ds(1, LON - 1)]
 
+    def receive(i, _):
+        k = lax.select(i == LEV - 1, LEV - 1, lax.select(i == LEV - 2, 0, i + 1))
+        pltpu.make_async_copy(D.at[k], D.at[k], br.at[k]).wait()
+
+        def unpack(n, _):
+            t, half = n // 2, n % 2
+            pieces = [
+                D[k, t, v // 2, pl.ds(8 * half, 8), (v % 2) * HALF : (v % 2 + 1) * HALF]
+                for v in range(2 * KEPT)
+            ]
+            pieces += [pieces[-1]] * (PIECES - 2 * KEPT)
+            for bit in reversed(range(BITS)):
+                far = 1 << bit
+                for v in reversed(range(far, PIECES)):
+                    pieces[v] = jnp.where(goes[bit * PIECES + v] > 0, pieces[v - far], pieces[v])
+            pieces = [along(pieces[v], scatter[v]) for v in range(PIECES)]
+            for group in range(2):
+                for side in range(2):
+                    lanes = slice(side * HALF, (side + 1) * HALF)
+                    block = jnp.stack([pieces[2 * (8 * group + j) + side] for j in range(8)])
+                    block = jnp.swapaxes(block, 0, 1)
+                    here = wat_v[8 * group : 8 * group + 8, lanes] > 0
+                    for d in range(8):
+                        at = (t, LEV * (8 * half + d) + k, pl.ds(8 * group, 8), lanes)
+                        sol_o[at] = jnp.where(here, block[d], sol_o[at])
+            return 0
+
+        lax.fori_loop(0, 4, unpack, 0)
+        return 0
+
+    original.wait()
+    lax.fori_loop(0, LEV, receive, 0)
+    packed = goes.at[pl.ds(0, 2 * (SECS - 1) * KEPT * LAT // (8 * HALF))]
+
     def finish(k, _):
         pltpu.make_async_copy(sent, sent, fs.at[k]).wait()
-        pltpu.make_async_copy(sent, sent, bs.at[k]).wait()
-        back = sol_o.at[0, pl.ds(0, 2 * SECS)]
-        pltpu.make_async_copy(back, back, br.at[k]).wait()
+        pltpu.make_async_copy(packed, packed, bs.at[k]).wait()
         return 0
 
     lax.fori_loop(0, LEV, finish, 0)
@@ -337,7 +445,13 @@
         out_specs=(vmem,) * 4,
         scratch_shapes=[
             pltpu.VMEM((LEV + 2, LON + 2, TR, LAT), F32),
-            pltpu.VMEM((LEV, LON, TR, LAT), F32),
+            pltpu.VMEM((LON, TR, LAT), F32),
+            pltpu.VMEM((LEV, KEPT, TR, LAT), F32),
+            pltpu.VMEM((LEV, 2, KEPT, SECS, LAT), F32),
+            pltpu.VMEM((BITS * PIECES, 8, HALF), jnp.int32),
+            pltpu.VMEM((BITS * PIECES, 8, HALF), jnp.int32),
+            pltpu.VMEM((PIECES, 8, HALF), jnp.int32),
+            pltpu.VMEM((PIECES, 8, HALF), jnp.int32),
             pltpu.VMEM((LEV, 7, LON, LAT), F32),
             pltpu.VMEM((2 * TR, LAT), BF16),
             pltpu.VMEM((2, LEV, LON, LAT), F32),
@@ -357,12 +471,13 @@
             pltpu.VMEM((LEV, LON, LAT), F32),
             pltpu.VMEM((SECS, LON, LAT), F32),
             pltpu.VMEM((LEV, LON, LAT), F32),
+            pltpu.VMEM((4, LON, LAT), jnp.int32),
             dma((8,)), dma((3,)), dma((5,)), dma((5,)),
             dma, dma((LEV,)), dma((LEV,)), dma((LEV,)), dma((2,)), dma((2,)), dma((LEV,)), dma((LEV,)),
             dma, dma, dma,
         ],
         compiler_params=pltpu.CompilerParams(
-            collective_id=0, has_side_effects=True, vmem_limit_bytes=28 << 20
+            collective_id=0, has_side_effects=True, vmem_limit_bytes=48 << 20
         ),
         name="ocean_step",
     )(*(pltpu.with_memory_space_constraint(a, pltpu.HBM) for a in given))

time: 126 us -> 121 us (0.960)
  Pallas kernels: 125 us -> 120 us
    pallas_call x1, Pallas kernels: 123 us -> 118 us  [on_device(): pl.pallas_call(kernel, out_shape=shapes, in_specs=[hbm] * 9, out_specs=(v...]
where the time goes in v3:
time: 121 us
  Pallas kernels  120 us (99%)
    pallas_call x1, Pallas kernels, on_device(): pl.pallas_call(kernel, out_shape=shapes, in_specs=[hbm] * 9, out_specs=(v...  118 us

profile of v3, /device:TPU:1, one launch (start us, length us, event | category | flops | bytes accessed | tf_op | source)
XLA Modules:
  0.0 120.6 jit_solution(1484346907155105136)
XLA Ops:
  0.6 117.8 %ocean_step.1 = (f32[8,16,256]{2,1,0:T(8,128)S(1)}, f32[2,8,16,256]{3,2,1,0:T(8,128)S(1)}, f32[8,16,256]{2,1,0:T(8,128)S(1)}, f32[2,128,16,256]{3,2,1,0:T(8,128)S(1)}) custom-call(f32[2,128,16,256]{3,2,1,0:T(8,128)} %x.1, f32[2,8,16,256]{3,2,1,0:T(8,128)} %flow.1, f32[8,16,256]{2,1,0:T(8,128)} %kap.1, f32[8,16,256]{2,1,0:T(8,128)} %th.1, f32[32,32]{1,0:T(8,128)} %lin.1, ...), custom_call_target="tpu_custom_call" | custom-call | tf_op jit(solution)/shard_map/ocean_step/pallas_call | solution.py:441
  118.4 2.2 %settle.1 = (f32[8,16,256]{2,1,0:T(8,128)}, f32[2,8,16,256]{3,2,1,0:T(8,128)}, f32[8,16,256]{2,1,0:T(8,128)}, f32[2,128,16,256]{3,2,1,0:T(8,128)}) custom-call(f32[8,16,256]{2,1,0:T(8,128)S(1)} %get-tuple-element.8.refs_0_, f32[2,8,16,256]{3,2,1,0:T(8,128)S(1)} %get-tuple-element.9.refs_1_, f32[8,16,256]{2,1,0:T(8,128)S(1)} %get-tuple-element.10.refs_2_, ...), custom_call_target="tpu_custom_call" | custom-call | tf_op jit(solution)/shard_map/settle/pallas_call | solution.py:484

commit v4 on v3

--- a/solution.py
+++ b/solution.py
@@ -100,7 +100,7 @@
             ).start()
 
         def peer(r, _):
-            d = s ^ r
+            d = (s + r) % SECS
             for t in range(2):
                 remote(
                     x.at[t, LEV * d + k], R.at[k + 1, pl.ds(1, LON), 2 * s + t, :],
@@ -310,6 +310,11 @@
         def _():
             arrived(i + 4, 0)
 
+        return 0
+
+    def give(i, _):
+        k = lax.select(i == LEV - 1, LEV - 1, lax.select(i == LEV - 2, 0, i + 1))
+
         def pack(g, _):
             pieces = [
                 along(S[v // 2, pl.ds(8 * g, 8), (v % 2) * HALF : (v % 2 + 1) * HALF], gather[v])
@@ -329,7 +334,7 @@
             pltpu.make_async_copy(C.at[k, :, 2 * s + t, :], D.at[k, t, :, s, :], br.at[k]).start()
 
         def peer(r, _):
-            d = s ^ r
+            d = (s + r) % SECS
             for t in range(2):
                 remote(
                     C.at[k, :, 2 * d + t, :], D.at[k, t, :, s, :], bs.at[k], br.at[k], (c, d)
@@ -340,7 +345,12 @@
 
         return 0
 
-    lax.fori_loop(0, LEV, level, 0)
+    def both_of(i, _):
+        level(i, 0)
+        return give(i, 0)
+
+    lax.fori_loop(0, LEV - 1, both_of, 0)
+    level(LEV - 1, 0)
 
     total = jnp.zeros((LON, LAT), F32)
     for k in range(LEV):
@@ -348,29 +358,11 @@
     totals[s] = total
 
     def tell(r, _):
-        remote(totals.at[s], totals.at[s], ts, tr_, (c, s ^ r)).start()
+        remote(totals.at[s], totals.at[s], ts, tr_, (c, (s + r) % SECS)).start()
         return 0
 
     lax.fori_loop(1, SECS, tell, 0)
-    others = totals.at[pl.ds(0, SECS - 1)]
-    pltpu.make_async_copy(others, others, tr_).wait()
-    depth = jnp.zeros((LON, LAT), F32)
-    for d in range(SECS):
-        depth += totals[d] * jnp.where(d < s, 1.0, 0.0)
-    light = CHLOROPHYLL_WARM * jnp.broadcast_to(lat_v[1:2, :], (LON, LAT)) * wet
-    before = jnp.exp(-depth)
-    for k in range(LEV):
-        depth = depth + (WATER_ABSORB + PIGMENT_ABSORB * saturating(pig[k]))
-        after = jnp.exp(-depth)
-        thn_v[k] = thn_v[k] + light * (before - after)
-        before = after
-    outs.append(pltpu.make_async_copy(thn_v, th_o, osem.at[2]))
-    outs[-1].start()
-
-    pltpu.make_async_copy(others, others, ts).wait()
-    pltpu.make_async_copy(edge, edge, hs).wait()
-    for copy in verticals:
-        copy.wait_send()
+    give(LEV - 1, 0)
     sent = R.at[1, pl.ds(1, LON - 1)]
 
     def receive(i, _):
@@ -404,7 +396,24 @@
         return 0
 
     original.wait()
-    lax.fori_loop(0, LEV, receive, 0)
+    lax.fori_loop(0, LEV - 1, receive, 0)
+
+    others = totals.at[pl.ds(0, SECS - 1)]
+    pltpu.make_async_copy(others, others, tr_).wait()
+    depth = jnp.zeros((LON, LAT), F32)
+    for d in range(SECS):
+        depth += totals[d] * jnp.where(d < s, 1.0, 0.0)
+    light = CHLOROPHYLL_WARM * jnp.broadcast_to(lat_v[1:2, :], (LON, LAT)) * wet
+    before = jnp.exp(-depth)
+    for k in range(LEV):
+        depth = depth + (WATER_ABSORB + PIGMENT_ABSORB * saturating(pig[k]))
+        after = jnp.exp(-depth)
+        thn_v[k] = thn_v[k] + light * (before - after)
+        before = after
+    outs.append(pltpu.make_async_copy(thn_v, th_o, osem.at[2]))
+    outs[-1].start()
+
+    receive(LEV - 1, 0)
     packed = goes.at[pl.ds(0, 2 * (SECS - 1) * KEPT * LAT // (8 * HALF))]
 
     def finish(k, _):
@@ -412,6 +421,10 @@
         pltpu.make_async_copy(packed, packed, bs.at[k]).wait()
         return 0
 
+    pltpu.make_async_copy(edge, edge, hs).wait()
+    for copy in verticals:
+        copy.wait_send()
+    pltpu.make_async_copy(others, others, ts).wait()
     lax.fori_loop(0, LEV, finish, 0)
     for copy in outs:
         copy.wait()

time: 121 us -> 114 us (0.942)
  Pallas kernels: 120 us -> 113 us
    pallas_call x1, Pallas kernels: 118 us -> 111 us  [on_device(): pl.pallas_call(kernel, out_shape=shapes, in_specs=[hbm] * 9, out_specs=(v...]
where the time goes in v4:
time: 114 us
  Pallas kernels  113 us (99%)
    pallas_call x1, Pallas kernels, on_device(): pl.pallas_call(kernel, out_shape=shapes, in_specs=[hbm] * 9, out_specs=(v...  111 us

profile of v4, /device:TPU:1, one launch (start us, length us, event | category | flops | bytes accessed | tf_op | source)
XLA Modules:
  0.0 113.6 jit_solution(14115600610738385020)
XLA Ops:
  0.6 110.7 %ocean_step.1 = (f32[8,16,256]{2,1,0:T(8,128)S(1)}, f32[2,8,16,256]{3,2,1,0:T(8,128)S(1)}, f32[8,16,256]{2,1,0:T(8,128)S(1)}, f32[2,128,16,256]{3,2,1,0:T(8,128)S(1)}) custom-call(f32[2,128,16,256]{3,2,1,0:T(8,128)} %x.1, f32[2,8,16,256]{3,2,1,0:T(8,128)} %flow.1, f32[8,16,256]{2,1,0:T(8,128)} %kap.1, f32[8,16,256]{2,1,0:T(8,128)} %th.1, f32[32,32]{1,0:T(8,128)} %lin.1, ...), custom_call_target="tpu_custom_call" | custom-call | tf_op jit(solution)/shard_map/ocean_step/pallas_call | solution.py:454
  111.4 2.2 %settle.1 = (f32[8,16,256]{2,1,0:T(8,128)}, f32[2,8,16,256]{3,2,1,0:T(8,128)}, f32[8,16,256]{2,1,0:T(8,128)}, f32[2,128,16,256]{3,2,1,0:T(8,128)}) custom-call(f32[8,16,256]{2,1,0:T(8,128)S(1)} %get-tuple-element.8.refs_0_, f32[2,8,16,256]{3,2,1,0:T(8,128)S(1)} %get-tuple-element.9.refs_1_, f32[8,16,256]{2,1,0:T(8,128)S(1)} %get-tuple-element.10.refs_2_, ...), custom_call_target="tpu_custom_call" | custom-call | tf_op jit(solution)/shard_map/settle/pallas_call | solution.py:497

commit v5 on v4

--- a/solution.py
+++ b/solution.py
@@ -19,7 +19,7 @@
 LON = 16
 TR = 32
 LAT = 256
-AHEAD = 4
+AHEAD = 2
 KEPT = 12
 BITS = 5
 HALF = 128
@@ -115,6 +115,16 @@
 
     original = pltpu.make_async_copy(x, sol_o, xs)
     original.start()
+
+    def blank(end):
+        def one(j, _):
+            R[end, j + 1] = jnp.zeros((TR, LAT), F32)
+            return 0
+
+        lax.fori_loop(0, LON, one, 0)
+
+    pl.when(s == 0)(lambda: blank(0))
+    pl.when(s == SECS - 1)(lambda: blank(LEV + 1))
 
     for copy in loads:
         copy.wait()
@@ -249,11 +259,11 @@
         remote(R.at[k + 1, 1], R.at[k + 1, LON + 1], hs, hr.at[k], (left, s)).start()
         remote(R.at[k + 1, LON], R.at[k + 1, 0], hs, hr.at[k], (right, s)).start()
 
-        @pl.when(i == 0)
+        @pl.when((i == 0) & (s > 0))
         def _():
             verticals[0].start()
 
-        @pl.when(i == 1)
+        @pl.when((i == 1) & (s < SECS - 1))
         def _():
             verticals[1].start()
 
@@ -274,11 +284,11 @@
         both = R.at[k + 1, pl.ds(0, 2)]
         pltpu.make_async_copy(both, both, hr.at[k]).wait()
 
-        @pl.when(i == LEV - 2)
+        @pl.when((i == LEV - 2) & (s > 0))
         def _():
             verticals[1].wait_recv()
 
-        @pl.when(i == LEV - 1)
+        @pl.when((i == LEV - 1) & (s < SECS - 1))
         def _():
             verticals[0].wait_recv()
 
@@ -422,8 +432,15 @@
         return 0
 
     pltpu.make_async_copy(edge, edge, hs).wait()
-    for copy in verticals:
-        copy.wait_send()
+
+    @pl.when(s > 0)
+    def _():
+        verticals[0].wait_send()
+
+    @pl.when(s < SECS - 1)
+    def _():
+        verticals[1].wait_send()
+
     pltpu.make_async_copy(others, others, ts).wait()
     lax.fori_loop(0, LEV, finish, 0)
     for copy in outs:

time: 114 us -> 113 us (level)
  no operation moved by 1% of the time
where the time goes in v5:
time: 113 us
  Pallas kernels  112 us (99%)
    pallas_call x1, Pallas kernels, on_device(): pl.pallas_call(kernel, out_shape=shapes, in_specs=[hbm] * 9, out_specs=(v...  110 us

profile of v5, /device:TPU:1, one launch (start us, length us, event | category | flops | bytes accessed | tf_op | source)
XLA Modules:
  0.0 112.5 jit_solution(6711759084050522462)
XLA Ops:
  0.6 109.7 %ocean_step.1 = (f32[8,16,256]{2,1,0:T(8,128)S(1)}, f32[2,8,16,256]{3,2,1,0:T(8,128)S(1)}, f32[8,16,256]{2,1,0:T(8,128)S(1)}, f32[2,128,16,256]{3,2,1,0:T(8,128)S(1)}) custom-call(f32[2,128,16,256]{3,2,1,0:T(8,128)} %x.1, f32[2,8,16,256]{3,2,1,0:T(8,128)} %flow.1, f32[8,16,256]{2,1,0:T(8,128)} %kap.1, f32[8,16,256]{2,1,0:T(8,128)} %th.1, f32[32,32]{1,0:T(8,128)} %lin.1, ...), custom_call_target="tpu_custom_call" | custom-call | tf_op jit(solution)/shard_map/ocean_step/pallas_call | solution.py:471
  110.3 2.2 %settle.1 = (f32[8,16,256]{2,1,0:T(8,128)}, f32[2,8,16,256]{3,2,1,0:T(8,128)}, f32[8,16,256]{2,1,0:T(8,128)}, f32[2,128,16,256]{3,2,1,0:T(8,128)}) custom-call(f32[8,16,256]{2,1,0:T(8,128)S(1)} %get-tuple-element.8.refs_0_, f32[2,8,16,256]{3,2,1,0:T(8,128)S(1)} %get-tuple-element.9.refs_1_, f32[8,16,256]{2,1,0:T(8,128)S(1)} %get-tuple-element.10.refs_2_, ...), custom_call_target="tpu_custom_call" | custom-call | tf_op jit(solution)/shard_map/settle/pallas_call | solution.py:514

commit v6 on v5

--- a/solution.py
+++ b/solution.py
@@ -50,7 +50,7 @@
     th_o, vel_o, kap_o, sol_o,
     R, S, C, D, comes, goes, gather, scatter, coef, lhs, flow_v, kap_v, th_v, lin_v, pre_v, ab_v, wat_v, lat_v,
     below_v, above_v, kabove_v, thh, vel_v, knext_v, pig, totals, thn_v, scr_v,
-    lsem, osem, small_s, small_r, hs, hr, fs, fr, vs, vr, bs, br, ts, tr_, xs,
+    lsem, osem, small_s, small_r, hs, hr, fs, fr, vs, vr, bs, br, ts, tr_, xs, VP, VQ,
 ):
     c = lax.axis_index("col")
     s = lax.axis_index("sec")
@@ -248,9 +248,49 @@
     def all_of(k, sem):
         pltpu.make_async_copy(R.at[k + 1, pl.ds(1, LON)], R.at[k + 1, pl.ds(1, LON)], sem).wait()
 
+    def places(g, first=0):
+        return [
+            (first + v // 2, pl.ds(pl.multiple_of(8 * g, 8), 8), slice((v % 2) * HALF, (v % 2 + 1) * HALF))
+            for v in range(PIECES)
+        ]
+
+    def packed(pieces):
+        pieces = [along(pieces[v], gather[v]) for v in range(PIECES)]
+        for bit in range(BITS):
+            far = 1 << bit
+            for v in range(PIECES - far):
+                pieces[v] = jnp.where(comes[bit * PIECES + v] > 0, pieces[v + far], pieces[v])
+        return pieces
+
+    def unpacked(pieces):
+        pieces = pieces + [pieces[-1]] * (PIECES - 2 * KEPT)
+        for bit in reversed(range(BITS)):
+            far = 1 << bit
+            for v in reversed(range(far, PIECES)):
+                pieces[v] = jnp.where(goes[bit * PIECES + v] > 0, pieces[v - far], pieces[v])
+        return [along(pieces[v], scatter[v]) for v in range(PIECES)]
+
+    def pack_level(held, end):
+        def one(g, _):
+            pieces = packed([R[(held,) + at] for at in places(g, 1)])
+            for at, piece in zip(places(g)[: 2 * KEPT], pieces):
+                VP[(end,) + at] = piece
+            return 0
+
+        lax.fori_loop(0, TR // 8, one, 0)
+
+    def unpack_level(end, held):
+        def one(g, _):
+            pieces = unpacked([VQ[(end,) + at] for at in places(g)[: 2 * KEPT]])
+            for at, piece in zip(places(g, 1), pieces):
+                R[(held,) + at] = piece
+            return 0
+
+        lax.fori_loop(0, TR // 8, one, 0)
+
     verticals = [
-        remote(R.at[1, pl.ds(1, LON)], R.at[LEV + 1, pl.ds(1, LON)], vs.at[0], vr.at[0], (c, up)),
-        remote(R.at[LEV, pl.ds(1, LON)], R.at[0, pl.ds(1, LON)], vs.at[1], vr.at[1], (c, down)),
+        remote(VP.at[0], VQ.at[1], vs.at[0], vr.at[0], (c, up)),
+        remote(VP.at[1], VQ.at[0], vs.at[1], vr.at[1], (c, down)),
     ]
 
     def arrived(i, _):
@@ -261,10 +301,12 @@
 
         @pl.when((i == 0) & (s > 0))
         def _():
+            pack_level(1, 0)
             verticals[0].start()
 
         @pl.when((i == 1) & (s < SECS - 1))
         def _():
+            pack_level(LEV, 1)
             verticals[1].start()
 
         @pl.when(i < LEV - AHEAD)
@@ -287,10 +329,12 @@
         @pl.when((i == LEV - 2) & (s > 0))
         def _():
             verticals[1].wait_recv()
+            unpack_level(0, 0)
 
         @pl.when((i == LEV - 1) & (s < SECS - 1))
         def _():
             verticals[0].wait_recv()
+            unpack_level(1, LEV + 1)
 
         def column(j, _):
             def row_of(n):
@@ -326,14 +370,7 @@
         k = lax.select(i == LEV - 1, LEV - 1, lax.select(i == LEV - 2, 0, i + 1))
 
         def pack(g, _):
-            pieces = [
-                along(S[v // 2, pl.ds(8 * g, 8), (v % 2) * HALF : (v % 2 + 1) * HALF], gather[v])
-                for v in range(PIECES)
-            ]
-            for bit in range(BITS):
-                far = 1 << bit
-                for v in range(PIECES - far):
-                    pieces[v] = jnp.where(comes[bit * PIECES + v] > 0, pieces[v + far], pieces[v])
+            pieces = packed([S[at] for at in places(g)])
             for v in range(2 * KEPT):
                 C[k, v // 2, pl.ds(8 * g, 8), (v % 2) * HALF : (v % 2 + 1) * HALF] = pieces[v]
             return 0
@@ -385,12 +422,7 @@
                 D[k, t, v // 2, pl.ds(8 * half, 8), (v % 2) * HALF : (v % 2 + 1) * HALF]
                 for v in range(2 * KEPT)
             ]
-            pieces += [pieces[-1]] * (PIECES - 2 * KEPT)
-            for bit in reversed(range(BITS)):
-                far = 1 << bit
-                for v in reversed(range(far, PIECES)):
-                    pieces[v] = jnp.where(goes[bit * PIECES + v] > 0, pieces[v - far], pieces[v])
-            pieces = [along(pieces[v], scatter[v]) for v in range(PIECES)]
+            pieces = unpacked(pieces)
             for group in range(2):
                 for side in range(2):
                     lanes = slice(side * HALF, (side + 1) * HALF)
@@ -505,6 +537,8 @@
             dma((8,)), dma((3,)), dma((5,)), dma((5,)),
             dma, dma((LEV,)), dma((LEV,)), dma((LEV,)), dma((2,)), dma((2,)), dma((LEV,)), dma((LEV,)),
             dma, dma, dma,
+            pltpu.VMEM((2, KEPT, TR, LAT), F32),
+            pltpu.VMEM((2, KEPT, TR, LAT), F32),
         ],
         compiler_params=pltpu.CompilerParams(
             collective_id=0, has_side_effects=True, vmem_limit_bytes=48 << 20

time: 113 us -> 111 us (0.982)
  Pallas kernels: 112 us -> 110 us
    pallas_call x1, Pallas kernels: 110 us -> 108 us  [on_device(): pl.pallas_call(kernel, out_shape=shapes, in_specs=[hbm] * 9, out_specs=(v...]
where the time goes in v6:
time: 111 us
  Pallas kernels  110 us (99%)
    pallas_call x1, Pallas kernels, on_device(): pl.pallas_call(kernel, out_shape=shapes, in_specs=[hbm] * 9, out_specs=(v...  108 us
    pallas_call x1, Pallas kernels, on_device(): pl.pallas_call(settle, out_shape=shapes, in_specs=[vmem] * 4, out_specs=(...  2.22 us

profile of v6, /device:TPU:1, one launch (start us, length us, event | category | flops | bytes accessed | tf_op | source)
XLA Modules:
  0.0 110.8 jit_solution(7838386394557124318)
XLA Ops:
  0.6 108.0 %ocean_step.1 = (f32[8,16,256]{2,1,0:T(8,128)S(1)}, f32[2,8,16,256]{3,2,1,0:T(8,128)S(1)}, f32[8,16,256]{2,1,0:T(8,128)S(1)}, f32[2,128,16,256]{3,2,1,0:T(8,128)S(1)}) custom-call(f32[2,128,16,256]{3,2,1,0:T(8,128)} %x.1, f32[2,8,16,256]{3,2,1,0:T(8,128)} %flow.1, f32[8,16,256]{2,1,0:T(8,128)} %kap.1, f32[8,16,256]{2,1,0:T(8,128)} %th.1, f32[32,32]{1,0:T(8,128)} %lin.1, ...), custom_call_target="tpu_custom_call" | custom-call | tf_op jit(solution)/shard_map/ocean_step/pallas_call | solution.py:503
  108.6 2.2 %settle.1 = (f32[8,16,256]{2,1,0:T(8,128)}, f32[2,8,16,256]{3,2,1,0:T(8,128)}, f32[8,16,256]{2,1,0:T(8,128)}, f32[2,128,16,256]{3,2,1,0:T(8,128)}) custom-call(f32[8,16,256]{2,1,0:T(8,128)S(1)} %get-tuple-element.8.refs_0_, f32[2,8,16,256]{3,2,1,0:T(8,128)S(1)} %get-tuple-element.9.refs_1_, f32[8,16,256]{2,1,0:T(8,128)S(1)} %get-tuple-element.10.refs_2_, ...), custom_call_target="tpu_custom_call" | custom-call | tf_op jit(solution)/shard_map/settle/pallas_call | solution.py:548

commit v7 on v6

--- a/solution.py
+++ b/solution.py
@@ -63,9 +63,6 @@
             [(flow, flow_v), (kap, kap_v), (th, th_v), (lin, lin_v), (pre, pre_v), (ab, ab_v), (wat, wat_v), (lat, lat_v)]
         )
     ]
-    for copy in loads:
-        copy.start()
-
     barrier = pltpu.get_barrier_semaphore()
 
     def greet(r, _):
@@ -75,6 +72,8 @@
     lax.fori_loop(1, SECS, greet, 0)
     pl.semaphore_signal(barrier, inc=1, device_id=(left, s), device_id_type=MESH)
     pl.semaphore_signal(barrier, inc=1, device_id=(right, s), device_id_type=MESH)
+    for copy in loads:
+        copy.start()
     pl.semaphore_wait(barrier, SECS + 1)
 
     def remote(src, dst, send, recv, to):

time: 111 us -> 111 us (level)
  no operation moved by 1% of the time
where the time goes in v7:
time: 111 us
  Pallas kernels  110 us (99%)
    pallas_call x1, Pallas kernels, on_device(): pl.pallas_call(kernel, out_shape=shapes, in_specs=[hbm] * 9, out_specs=(v...  108 us
    pallas_call x1, Pallas kernels, on_device(): pl.pallas_call(settle, out_shape=shapes, in_specs=[vmem] * 4, out_specs=(...  2.22 us

profile of v7, /device:TPU:1, one launch (start us, length us, event | category | flops | bytes accessed | tf_op | source)
XLA Modules:
  0.0 110.8 jit_solution(1558049432738849847)
XLA Ops:
  0.6 108.0 %ocean_step.1 = (f32[8,16,256]{2,1,0:T(8,128)S(1)}, f32[2,8,16,256]{3,2,1,0:T(8,128)S(1)}, f32[8,16,256]{2,1,0:T(8,128)S(1)}, f32[2,128,16,256]{3,2,1,0:T(8,128)S(1)}) custom-call(f32[2,128,16,256]{3,2,1,0:T(8,128)} %x.1, f32[2,8,16,256]{3,2,1,0:T(8,128)} %flow.1, f32[8,16,256]{2,1,0:T(8,128)} %kap.1, f32[8,16,256]{2,1,0:T(8,128)} %th.1, f32[32,32]{1,0:T(8,128)} %lin.1, ...), custom_call_target="tpu_custom_call" | custom-call | tf_op jit(solution)/shard_map/ocean_step/pallas_call | solution.py:502
  108.6 2.2 %settle.1 = (f32[8,16,256]{2,1,0:T(8,128)}, f32[2,8,16,256]{3,2,1,0:T(8,128)}, f32[8,16,256]{2,1,0:T(8,128)}, f32[2,128,16,256]{3,2,1,0:T(8,128)}) custom-call(f32[8,16,256]{2,1,0:T(8,128)S(1)} %get-tuple-element.8.refs_0_, f32[2,8,16,256]{3,2,1,0:T(8,128)S(1)} %get-tuple-element.9.refs_1_, f32[8,16,256]{2,1,0:T(8,128)S(1)} %get-tuple-element.10.refs_2_, ...), custom_call_target="tpu_custom_call" | custom-call | tf_op jit(solution)/shard_map/settle/pallas_call | solution.py:547
